TPU v7x, 32 devices: a whole 2x2x4 slice. The times are simulated.
32 devices in a mesh: node: 8 (over z, y), col: 4 (over x, core).
Axes of the slice: x: 2, y: 2, z: 4, core: 2. Of those that a mesh axis runs over, the one named last changes fastest.
Arguments:
- blocks: float32 [2304, 128, 128], P('node'), may hold values from 0.001 to 1
- owner_row: int32 [8, 288], P('node'), may hold values from 0 to 47, never falling along the last dimension, each value on 1 to 10 neighbouring positions
- block_col: int32 [8, 288], P('node'), may hold values from 0 to 383, as said below
- start: float32 [128, 49152], P('col', 'node'), may hold values from -160 to 160
Outputs:
- basis: float32 [128, 49152], P('col', 'node')
- projected_first: float32 [128, 128], P('col')
- projected: float32 [128, 128], P('col')
Inputs may be any that keep to these rules, and one draw needn't show every extreme that they name: `owner_row`: the stored blocks of one index of node are listed by block row, never falling; every block row has 1 to 10 stored blocks, one has exactly 10. `block_col`: A block stored at index g of node has its block column among the block rows of index g, among the last 24 block rows of index g - 1, or among the first 24 block rows of index g + 1, cyclically over node; every index has blocks at both of those bounds.
All inputs are finite; a program needn't handle non-finite values.
Results may differ from a plain program's by a relative error of at most 0.0003.
Values sent between devices are 32-bit elements; how exact they have to be, the bound alone decides.
No kernel may reach another device: no remote copies, remote signals or barrier semaphores. Data moves between devices by JAX's collectives and lax.ppermute only.
A program may use at most 128 MiB of HBM per device.

v0:
```python
import jax
import jax.numpy as jnp
from jax import lax
from jax.sharding import PartitionSpec as P

DEGREE = 4
ITERS = 2
precise = lax.Precision.HIGHEST
center = 1.025
half_width = 0.975


def extended_2(cells, sides, width):
    for axis, dim in sides:
        count = lax.axis_size(axis)
        head = lax.slice_in_dim(cells, 0, width, axis=dim)
        tail = lax.slice_in_dim(cells, cells.shape[dim] - width, cells.shape[dim], axis=dim)
        cells = jnp.concatenate(
            [
                lax.ppermute(tail, axis, [(i, (i + 1) % count) for i in range(count)]),
                cells,
                lax.ppermute(head, axis, [((i + 1) % count, i) for i in range(count)]),
            ],
            axis=dim,
        )
    return cells


def chebyshev(panel, operate):
    previous = panel
    current = (operate(panel) - center * panel) / half_width
    for step in range(DEGREE - 1):
        following = 2.0 * (operate(current) - center * current) / half_width - previous
        previous = current
        current = following
    return current


def body(blocks, owner_row, block_col, start):
    cols_here = start.shape[0]
    width = start.shape[1]
    block = blocks.shape[1]
    rows_blocks = width // block
    groups = lax.axis_size("node")
    nodes = width * groups
    row_ids = owner_row[0]
    col_ids = block_col[0]
    onehot = (row_ids[None, :] == jnp.arange(rows_blocks, dtype=jnp.int32)[:, None]).astype(
        jnp.float32
    )
    degree = jnp.einsum("rn,ni->ri", onehot, jnp.sum(blocks, axis=2), precision=precise).reshape(
        width
    )
    node_me = lax.axis_index("node")
    owner = col_ids // rows_blocks
    side = (owner - node_me + 1) % groups
    lookup = (side - 1) * rows_blocks + col_ids % rows_blocks + rows_blocks
    col_me = lax.axis_index("col")

    def operate(panel):
        extended = extended_2(panel, (("node", 1),), rows_blocks * block)
        pieces = extended.reshape(cols_here, -1, block)
        gathered = jnp.take(pieces, lookup, axis=1)
        product = jnp.einsum("nij,knj->nki", blocks, gathered, precision=precise)
        summed = jnp.einsum("rn,nki->kri", onehot, product, precision=precise).reshape(
            cols_here, width
        )
        return panel - summed / degree[None, :]

    def to_rows(panel):
        return lax.all_to_all(panel, "col", split_axis=1, concat_axis=0, tiled=True)

    basis = start
    results = []
    for step in range(ITERS):
        filtered = chebyshev(basis, operate)
        rows_now = to_rows(filtered)
        gram_part = jnp.dot(rows_now, rows_now.T, precision=precise) / nodes
        gram = lax.psum(gram_part, ("node", "col"))
        factor = jnp.linalg.cholesky(gram)
        rows_basis = jax.scipy.linalg.solve_triangular(factor, rows_now, lower=True)
        basis = lax.all_to_all(rows_basis, "col", split_axis=0, concat_axis=1, tiled=True)
        image = to_rows(operate(basis))
        part = jnp.dot(rows_basis, image.T, precision=precise) / nodes
        totals = lax.psum((part,), ("node", "col"))
        results.append(
            tuple(
                (
                    lax.dynamic_slice_in_dim(total, col_me * cols_here, cols_here, 0)
                    for total in totals
                )
            )[0]
        )
    return (basis, results[0], results[-1])


def solution(mesh):
    placed = (P("node", None, None), P("node", None), P("node", None), P("col", "node"))
    return jax.shard_map(
        body,
        mesh=mesh,
        in_specs=placed,
        out_specs=(P("col", "node"), P("col", None), P("col", None)),
        check_vma=False,
    )
```

profile of v0, /device:TPU:0, one launch (start us, length us, event | category | flops | bytes accessed | tf_op | source)
XLA Modules:
  0.0 1225.8 jit_solution(599584303518014007)
XLA Ops:
  14.1 9.6 reduce_sum.9
  23.9 20.3 %collective-permute-done = f32[32,6144]{1,0:T(8,128)S(1)} collective-permute-done((f32[32,6144]{1,0:T(8,128)}, f32[32,6144]{1,0:T(8,128)S(1)}, u32[]{:S(2)}, u32[]{:S(2)}) %collective-permute-start) | collective-permute-done | bytes 786464 | tf_op jit(solution)/shard_map/ppermute | solution.py:20
  51.4 33.1 %fusion.16 = f32[288,32,128]{2,1,0:T(8,128)S(1)} fusion(f32[288,128,128]{2,1,0:T(8,128)} %param.9, f32[288,32,128]{2,1,0:T(8,128)} %gather_fusion, pred[288]{0:T(512)(128)(4,1)S(1)} %get-tuple-element.25), kind=kOutput, calls=%fused_computation.25 | convolution fusion | flops 1813118976 | bytes 28311840 | tf_op jit(solution)/shard_map/nij,knj->nki/dot_general | solution.py:64
  94.4 29.1 %collective-permute-done.2 = f32[32,6144]{1,0:T(8,128)S(1)} collective-permute-done((f32[32,6144]{1,0:T(8,128)S(1)}, f32[32,6144]{1,0:T(8,128)S(1)}, u32[]{:S(2)}, u32[]{:S(2)}) %collective-permute-start.2) | collective-permute-done | bytes 786464 | tf_op jit(solution)/shard_map/ppermute | solution.py:20
  130.3 33.2 %fusion.14 = f32[288,32,128]{2,1,0:T(8,128)S(1)} fusion(f32[288,128,128]{2,1,0:T(8,128)} %param.9, f32[288,32,128]{2,1,0:T(8,128)} %gather_fusion.1, pred[288]{0:T(512)(128)(4,1)S(1)} %get-tuple-element.25), kind=kOutput, calls=%fused_computation.23 | convolution fusion | flops 1813118976 | bytes 28311840 | tf_op jit(solution)/shard_map/nij,knj->nki/dot_general | solution.py:64
  173.8 28.7 %collective-permute-done.4 = f32[32,6144]{1,0:T(8,128)S(1)} collective-permute-done((f32[32,6144]{1,0:T(8,128)S(1)}, f32[32,6144]{1,0:T(8,128)S(1)}, u32[]{:S(2)}, u32[]{:S(2)}) %collective-permute-start.4) | collective-permute-done | bytes 786464 | tf_op jit(solution)/shard_map/ppermute | solution.py:20
  210.2 33.4 %fusion.12 = f32[288,32,128]{2,1,0:T(8,128)S(1)} fusion(f32[288,128,128]{2,1,0:T(8,128)} %param.9, f32[288,32,128]{2,1,0:T(8,128)} %gather_fusion.2, pred[288]{0:T(512)(128)(4,1)S(1)} %get-tuple-element.25), kind=kOutput, calls=%fused_computation.21 | convolution fusion | flops 1813118976 | bytes 28311840 | tf_op jit(solution)/shard_map/nij,knj->nki/dot_general | solution.py:64
  253.9 28.5 %collective-permute-done.6 = f32[32,6144]{1,0:T(8,128)S(1)} collective-permute-done((f32[32,6144]{1,0:T(8,128)S(1)}, f32[32,6144]{1,0:T(8,128)S(1)}, u32[]{:S(2)}, u32[]{:S(2)}) %collective-permute-start.6) | collective-permute-done | bytes 786464 | tf_op jit(solution)/shard_map/ppermute | solution.py:20
  290.2 33.2 %fusion.10 = f32[288,32,128]{2,1,0:T(8,128)S(1)} fusion(f32[288,128,128]{2,1,0:T(8,128)} %param.9, f32[288,32,128]{2,1,0:T(8,128)} %gather_fusion.3, pred[288]{0:T(512)(128)(4,1)S(1)} %get-tuple-element.25), kind=kOutput, calls=%fused_computation.19 | convolution fusion | flops 1813118976 | bytes 28311840 | tf_op jit(solution)/shard_map/nij,knj->nki/dot_general | solution.py:64
  328.6 14.2 %all_to_all.105 = f32[32,4,1536]{2,0,1:T(8,128)S(1)} all-to-all(f32[32,4,1536]{2,0,1:T(8,128)S(1)} %bitcast.287), channel_id=1, replica_groups=mesh['node'=8,'col'=4] {'col'}, dimensions={1} | all-to-all | bytes 1572864 | tf_op jit(solution)/shard_map/all_to_all | solution.py:71
  344.6 114.6 %all-reduce.5.cloned.1.call-done = f32[128,128]{0,1:T(8,128)} async-done(((f32[128,128]{0,1:T(8,128)}), f32[128,128]{0,1:T(8,128)}) %all-reduce.5.cloned.1.call-update) | async-done | bytes 65552 | tf_op jit(solution)/shard_map/psum | solution.py:79
  461.0 11.7 cholesky.44
  474.1 9.8 custom-call.6
  484.7 15.4 %all_to_all.106 = f32[4,32,1536]{2,1,0:T(8,128)S(1)} all-to-all(f32[4,32,1536]{2,1,0:T(8,128)S(1)} %bitcast.280), channel_id=1, replica_groups=mesh['node'=8,'col'=4] {'col'}, dimensions={0} | all-to-all | bytes 1572864 | tf_op jit(solution)/shard_map/all_to_all | solution.py:82
  506.5 27.8 %collective-permute-done.8 = f32[32,6144]{1,0:T(8,128)} collective-permute-done((f32[32,6144]{1,0:T(8,128)S(1)}, f32[32,6144]{1,0:T(8,128)}, u32[]{:S(2)}, u32[]{:S(2)}) %collective-permute-start.8) | collective-permute-done | bytes 786464 | tf_op jit(solution)/shard_map/ppermute | solution.py:20
  541.1 33.1 %fusion.8 = f32[288,32,128]{2,1,0:T(8,128)S(1)} fusion(f32[288,128,128]{2,1,0:T(8,128)} %param.9, f32[288,32,128]{2,1,0:T(8,128)} %gather_fusion.4, pred[288]{0:T(512)(128)(4,1)S(1)} %get-tuple-element.25), kind=kOutput, calls=%fused_computation.17 | convolution fusion | flops 1813118976 | bytes 28311840 | tf_op jit(solution)/shard_map/nij,knj->nki/dot_general | solution.py:64
  584.1 28.3 %collective-permute-done.10 = f32[32,6144]{1,0:T(8,128)S(1)} collective-permute-done((f32[32,6144]{1,0:T(8,128)S(1)}, f32[32,6144]{1,0:T(8,128)S(1)}, u32[]{:S(2)}, u32[]{:S(2)}) %collective-permute-start.10) | collective-permute-done | bytes 786464 | tf_op jit(solution)/shard_map/ppermute | solution.py:20
  620.0 33.2 %fusion.6 = f32[288,32,128]{2,1,0:T(8,128)S(1)} fusion(f32[288,128,128]{2,1,0:T(8,128)} %param.9, f32[288,32,128]{2,1,0:T(8,128)} %gather_fusion.5, pred[288]{0:T(512)(128)(4,1)S(1)} %get-tuple-element.25), kind=kOutput, calls=%fused_computation.15 | convolution fusion | flops 1813118976 | bytes 28311840 | tf_op jit(solution)/shard_map/nij,knj->nki/dot_general | solution.py:64
  653.2 4.8 fusion.24
  663.5 28.5 %collective-permute-done.12 = f32[32,6144]{1,0:T(8,128)S(1)} collective-permute-done((f32[32,6144]{1,0:T(8,128)S(1)}, f32[32,6144]{1,0:T(8,128)S(1)}, u32[]{:S(2)}, u32[]{:S(2)}) %collective-permute-start.12) | collective-permute-done | bytes 786464 | tf_op jit(solution)/shard_map/ppermute | solution.py:20
  698.7 33.5 %fusion.4 = f32[288,32,128]{2,1,0:T(8,128)S(1)} fusion(f32[288,128,128]{2,1,0:T(8,128)} %param.9, f32[288,32,128]{2,1,0:T(8,128)} %gather_fusion.6, pred[288]{0:T(512)(128)(4,1)S(1)} %get-tuple-element.25), kind=kOutput, calls=%fused_computation.13 | convolution fusion | flops 1813118976 | bytes 28311840 | tf_op jit(solution)/shard_map/nij,knj->nki/dot_general | solution.py:64
  745.4 25.3 %collective-permute-done.14 = f32[32,6144]{1,0:T(8,128)} collective-permute-done((f32[32,6144]{1,0:T(8,128)S(1)}, f32[32,6144]{1,0:T(8,128)}, u32[]{:S(2)}, u32[]{:S(2)}) %collective-permute-start.14) | collective-permute-done | bytes 786464 | tf_op jit(solution)/shard_map/ppermute | solution.py:20
  779.6 33.2 %fusion.2 = f32[288,32,128]{2,1,0:T(8,128)S(1)} fusion(f32[288,128,128]{2,1,0:T(8,128)} %param.9, f32[288,32,128]{2,1,0:T(8,128)} %gather_fusion.7, pred[288]{0:T(512)(128)(4,1)S(1)} %get-tuple-element.25), kind=kOutput, calls=%fused_computation.11 | convolution fusion | flops 1813118976 | bytes 28311840 | tf_op jit(solution)/shard_map/nij,knj->nki/dot_general | solution.py:64
  822.3 14.7 %all_to_all.107 = f32[32,4,1536]{2,0,1:T(8,128)S(1)} all-to-all(f32[32,4,1536]{2,0,1:T(8,128)S(1)} %get-tuple-element.28), channel_id=1, replica_groups=mesh['node'=8,'col'=4] {'col'}, dimensions={1} | all-to-all | bytes 1572864 | tf_op jit(solution)/shard_map/all_to_all | solution.py:71
  838.4 115.4 %all-reduce.7.cloned.1.call-done = f32[128,128]{0,1:T(8,128)} async-done(((f32[128,128]{0,1:T(8,128)}), f32[128,128]{0,1:T(8,128)}) %all-reduce.7.cloned.1.call-update) | async-done | bytes 65552 | tf_op jit(solution)/shard_map/psum | solution.py:79
  955.6 11.7 cholesky.55
  968.7 9.8 custom-call.7
  979.3 15.4 %all_to_all.108 = f32[4,32,1536]{2,1,0:T(8,128)S(1)} all-to-all(f32[4,32,1536]{2,1,0:T(8,128)S(1)} %bitcast.281), channel_id=1, replica_groups=mesh['node'=8,'col'=4] {'col'}, dimensions={0} | all-to-all | bytes 1572864 | tf_op jit(solution)/shard_map/all_to_all | solution.py:82
  1004.3 27.4 %collective-permute-done.17 = f32[32,6144]{1,0:T(8,128)} collective-permute-done((f32[32,6144]{1,0:T(8,128)}, f32[32,6144]{1,0:T(8,128)}, u32[]{:S(2)}, u32[]{:S(2)}) %collective-permute-start.17) | collective-permute-done | bytes 786464 | tf_op jit(solution)/shard_map/ppermute | solution.py:22
  1037.7 33.1 %fusion = f32[288,32,128]{2,1,0:T(8,128)S(1)} fusion(f32[288,128,128]{2,1,0:T(8,128)} %param.9, f32[288,32,128]{2,1,0:T(8,128)} %gather_fusion.8, pred[288]{0:T(512)(128)(4,1)S(1)} %get-tuple-element.25), kind=kOutput, calls=%fused_computation.9 | convolution fusion | flops 1813118976 | bytes 28311840 | tf_op jit(solution)/shard_map/nij,knj->nki/dot_general | solution.py:64
  1085.3 9.0 all-to-all-done.5
  1095.7 121.1 %all-reduce.9.cloned.1.call-done = (f32[128,128]{0,1:T(8,128)}, f32[128,128]{0,1:T(8,128)}) async-done(((f32[128,128]{0,1:T(8,128)}, f32[128,128]{0,1:T(8,128)}), (f32[128,128]{0,1:T(8,128)}, f32[128,128]{0,1:T(8,128)})) %all-reduce.9.cloned.1.call-update) | async-done | bytes 131088 | tf_op jit(solution)/shard_map/psum | solution.py:85
  (165 shorter events, 191.2 us)
Async XLA Ops:
  7.2 452.0 %all-reduce.5.cloned.1.call-start = ((), (), s32[]{:S(2)}) async-start(), calls=%async_computation.6 | async-start | bytes 131072 | tf_op jit(solution)/shard_map/psum | solution.py:79
  7.2 37.0 %collective-permute-start = (f32[32,6144]{1,0:T(8,128)}, f32[32,6144]{1,0:T(8,128)S(1)}, u32[]{:S(2)}, u32[]{:S(2)}) collective-permute-start(f32[32,6144]{1,0:T(8,128)} %param.12), channel_id=1, source_target_pairs={{0,4},{4,8},{8,12},{12,16},{16,20},{20,24},{24,28},{28,0},{1,5},{5... | collective-permute-start | bytes 2359304 | tf_op jit(solution)/shard_map/ppermute | solution.py:20
  10.2 36.2 %collective-permute-start.1 = (f32[32,6144]{1,0:T(8,128)}, f32[32,6144]{1,0:T(8,128)}, u32[]{:S(2)}, u32[]{:S(2)}) collective-permute-start(f32[32,6144]{1,0:T(8,128)} %param.12), channel_id=1, source_target_pairs={{4,0},{8,4},{12,8},{16,12},{20,16},{24,20},{28,24},{0,28},{5,1},{9... | collective-permute-start | bytes 2359304 | tf_op jit(solution)/shard_map/ppermute | solution.py:22
  14.0 32.4 %copy-start = (f32[32,6144]{1,0:T(8,128)S(1)}, f32[32,6144]{1,0:T(8,128)}, u32[]{:S(2)}) copy-start(f32[32,6144]{1,0:T(8,128)} %param.12) | copy-start | bytes 2359300
  89.3 34.3 %copy-start.7 = (f32[32,128,48]{1,2,0:T(8,128)}, f32[32,128,48]{1,2,0:T(8,128)S(1)}, u32[]{:S(2)}) copy-start(f32[32,128,48]{1,2,0:T(8,128)S(1)} %fusion.34) | copy-start | bytes 2359300
  89.7 33.9 %collective-permute-start.2 = (f32[32,6144]{1,0:T(8,128)S(1)}, f32[32,6144]{1,0:T(8,128)S(1)}, u32[]{:S(2)}, u32[]{:S(2)}) collective-permute-start(f32[32,6144]{1,0:T(8,128)S(1)} %broadcast_multiply_fusion.1), channel_id=1, source_target_pairs={{0,4},{4,8},{8,12},{12,16},{16,20},{20,24},{24,28},{28,0},{1,5},{5... | collective-permute-start | bytes 2359304 | tf_op jit(solution)/shard_map/ppermute | solution.py:20
  90.8 35.9 %collective-permute-start.3 = (f32[32,6144]{1,0:T(8,128)S(1)}, f32[32,6144]{1,0:T(8,128)S(1)}, u32[]{:S(2)}, u32[]{:S(2)}) collective-permute-start(f32[32,6144]{1,0:T(8,128)S(1)} %broadcast_multiply_fusion.1), channel_id=1, source_target_pairs={{4,0},{8,4},{12,8},{16,12},{20,16},{24,20},{28,24},{0,28},{5,1},{9... | collective-permute-start | bytes 2359304 | tf_op jit(solution)/shard_map/ppermute | solution.py:22
  169.0 37.3 %copy-start.10 = (f32[32,6144]{1,0:T(8,128)}, f32[32,6144]{1,0:T(8,128)S(1)}, u32[]{:S(2)}) copy-start(f32[32,6144]{1,0:T(8,128)S(1)} %fusion.90) | copy-start | bytes 2359300
  169.0 33.5 %collective-permute-start.4 = (f32[32,6144]{1,0:T(8,128)S(1)}, f32[32,6144]{1,0:T(8,128)S(1)}, u32[]{:S(2)}, u32[]{:S(2)}) collective-permute-start(f32[32,6144]{1,0:T(8,128)S(1)} %fusion.90), channel_id=1, source_target_pairs={{0,4},{4,8},{8,12},{12,16},{16,20},{20,24},{24,28},{28,0},{1,5},{5... | collective-permute-start | bytes 2359304 | tf_op jit(solution)/shard_map/ppermute | solution.py:20
  169.1 37.2 %collective-permute-start.5 = (f32[32,6144]{1,0:T(8,128)S(1)}, f32[32,6144]{1,0:T(8,128)S(1)}, u32[]{:S(2)}, u32[]{:S(2)}) collective-permute-start(f32[32,6144]{1,0:T(8,128)S(1)} %fusion.90), channel_id=1, source_target_pairs={{4,0},{8,4},{12,8},{16,12},{20,16},{24,20},{28,24},{0,28},{5,1},{9... | collective-permute-start | bytes 2359304 | tf_op jit(solution)/shard_map/ppermute | solution.py:22
  249.1 37.3 %copy-start.19 = (f32[32,6144]{1,0:T(8,128)}, f32[32,6144]{1,0:T(8,128)S(1)}, u32[]{:S(2)}) copy-start(f32[32,6144]{1,0:T(8,128)S(1)} %fusion.86) | copy-start | bytes 2359300
  249.1 33.3 %collective-permute-start.6 = (f32[32,6144]{1,0:T(8,128)S(1)}, f32[32,6144]{1,0:T(8,128)S(1)}, u32[]{:S(2)}, u32[]{:S(2)}) collective-permute-start(f32[32,6144]{1,0:T(8,128)S(1)} %fusion.86), channel_id=1, source_target_pairs={{0,4},{4,8},{8,12},{12,16},{16,20},{20,24},{24,28},{28,0},{1,5},{5... | collective-permute-start | bytes 2359304 | tf_op jit(solution)/shard_map/ppermute | solution.py:20
  249.2 37.2 %collective-permute-start.7 = (f32[32,6144]{1,0:T(8,128)S(1)}, f32[32,6144]{1,0:T(8,128)S(1)}, u32[]{:S(2)}, u32[]{:S(2)}) collective-permute-start(f32[32,6144]{1,0:T(8,128)S(1)} %fusion.86), channel_id=1, source_target_pairs={{4,0},{8,4},{12,8},{16,12},{20,16},{24,20},{28,24},{0,28},{5,1},{9... | collective-permute-start | bytes 2359304 | tf_op jit(solution)/shard_map/ppermute | solution.py:22
  344.3 609.5 %all-reduce.7.cloned.1.call-start = ((), (), s32[]{:S(2)}) async-start(), calls=%async_computation.7 | async-start | bytes 131072 | tf_op jit(solution)/shard_map/psum | solution.py:79
  500.2 37.3 %copy-start.3 = (f32[4,4,8,1536]{3,2,0,1:T(8,128)}, f32[4,4,8,1536]{3,2,0,1:T(8,128)S(1)}, u32[]{:S(2)}) copy-start(f32[4,4,8,1536]{3,2,0,1:T(8,128)S(1)} %copy.168) | copy-start | bytes 2359300
  500.2 34.1 %collective-permute-start.8 = (f32[32,6144]{1,0:T(8,128)S(1)}, f32[32,6144]{1,0:T(8,128)}, u32[]{:S(2)}, u32[]{:S(2)}) collective-permute-start(f32[32,6144]{1,0:T(8,128)S(1)} %bitcast.269), channel_id=1, source_target_pairs={{0,4},{4,8},{8,12},{12,16},{16,20},{20,24},{24,28},{28,0},{1,5},{5... | collective-permute-start | bytes 2359304 | tf_op jit(solution)/shard_map/ppermute | solution.py:20
  501.0 36.4 %collective-permute-start.9 = (f32[32,6144]{1,0:T(8,128)S(1)}, f32[32,6144]{1,0:T(8,128)S(1)}, u32[]{:S(2)}, u32[]{:S(2)}) collective-permute-start(f32[32,6144]{1,0:T(8,128)S(1)} %bitcast.270), channel_id=1, source_target_pairs={{4,0},{8,4},{12,8},{16,12},{20,16},{24,20},{28,24},{0,28},{5,1},{9... | collective-permute-start | bytes 2359304 | tf_op jit(solution)/shard_map/ppermute | solution.py:22
  579.3 33.1 %collective-permute-start.10 = (f32[32,6144]{1,0:T(8,128)S(1)}, f32[32,6144]{1,0:T(8,128)S(1)}, u32[]{:S(2)}, u32[]{:S(2)}) collective-permute-start(f32[32,6144]{1,0:T(8,128)S(1)} %broadcast_multiply_fusion), channel_id=1, source_target_pairs={{0,4},{4,8},{8,12},{12,16},{16,20},{20,24},{24,28},{28,0},{1,5},{5... | collective-permute-start | bytes 2359304 | tf_op jit(solution)/shard_map/ppermute | solution.py:20
  580.1 36.1 %collective-permute-start.11 = (f32[32,6144]{1,0:T(8,128)S(1)}, f32[32,6144]{1,0:T(8,128)S(1)}, u32[]{:S(2)}, u32[]{:S(2)}) collective-permute-start(f32[32,6144]{1,0:T(8,128)S(1)} %broadcast_multiply_fusion), channel_id=1, source_target_pairs={{4,0},{8,4},{12,8},{16,12},{20,16},{24,20},{28,24},{0,28},{5,1},{9... | collective-permute-start | bytes 2359304 | tf_op jit(solution)/shard_map/ppermute | solution.py:22
  658.0 34.0 %copy-start.13 = (f32[32,128,48]{1,2,0:T(8,128)}, f32[32,128,48]{1,2,0:T(8,128)S(1)}, u32[]{:S(2)}) copy-start(f32[32,128,48]{1,2,0:T(8,128)S(1)} %fusion.24) | copy-start | bytes 2359300
  658.7 33.2 %collective-permute-start.12 = (f32[32,6144]{1,0:T(8,128)S(1)}, f32[32,6144]{1,0:T(8,128)S(1)}, u32[]{:S(2)}, u32[]{:S(2)}) collective-permute-start(f32[32,6144]{1,0:T(8,128)S(1)} %fusion.76), channel_id=1, source_target_pairs={{0,4},{4,8},{8,12},{12,16},{16,20},{20,24},{24,28},{28,0},{1,5},{5... | collective-permute-start | bytes 2359304 | tf_op jit(solution)/shard_map/ppermute | solution.py:20
  658.8 36.0 %collective-permute-start.13 = (f32[32,6144]{1,0:T(8,128)S(1)}, f32[32,6144]{1,0:T(8,128)S(1)}, u32[]{:S(2)}, u32[]{:S(2)}) collective-permute-start(f32[32,6144]{1,0:T(8,128)S(1)} %fusion.76), channel_id=1, source_target_pairs={{4,0},{8,4},{12,8},{16,12},{20,16},{24,20},{28,24},{0,28},{5,1},{9... | collective-permute-start | bytes 2359304 | tf_op jit(solution)/shard_map/ppermute | solution.py:22
  738.1 32.6 %copy-start.21 = (f32[32,6144]{1,0:T(8,128)}, f32[32,6144]{1,0:T(8,128)S(1)}, u32[]{:S(2)}) copy-start(f32[32,6144]{1,0:T(8,128)S(1)} %fusion.72) | copy-start | bytes 2359300
  738.1 32.6 %collective-permute-start.14 = (f32[32,6144]{1,0:T(8,128)S(1)}, f32[32,6144]{1,0:T(8,128)}, u32[]{:S(2)}, u32[]{:S(2)}) collective-permute-start(f32[32,6144]{1,0:T(8,128)S(1)} %fusion.72), channel_id=1, source_target_pairs={{0,4},{4,8},{8,12},{12,16},{16,20},{20,24},{24,28},{28,0},{1,5},{5... | collective-permute-start | bytes 2359304 | tf_op jit(solution)/shard_map/ppermute | solution.py:20
  738.1 36.1 %collective-permute-start.15 = (f32[32,6144]{1,0:T(8,128)S(1)}, f32[32,6144]{1,0:T(8,128)}, u32[]{:S(2)}, u32[]{:S(2)}) collective-permute-start(f32[32,6144]{1,0:T(8,128)S(1)} %fusion.72), channel_id=1, source_target_pairs={{4,0},{8,4},{12,8},{16,12},{20,16},{24,20},{28,24},{0,28},{5,1},{9... | collective-permute-start | bytes 2359304 | tf_op jit(solution)/shard_map/ppermute | solution.py:22
  979.3 25.0 %copy-start.17 = (f32[128,1536]{1,0:T(8,128)}, f32[128,1536]{1,0:T(8,128)S(1)}, u32[]{:S(2)}) copy-start(f32[128,1536]{1,0:T(8,128)S(1)} %fusion.120) | copy-start | bytes 2359300
  995.7 36.1 %collective-permute-start.17 = (f32[32,6144]{1,0:T(8,128)}, f32[32,6144]{1,0:T(8,128)}, u32[]{:S(2)}, u32[]{:S(2)}) collective-permute-start(f32[32,6144]{1,0:T(8,128)} %bitcast.69), channel_id=1, source_target_pairs={{4,0},{8,4},{12,8},{16,12},{20,16},{24,20},{28,24},{0,28},{5,1},{9... | collective-permute-start | bytes 2359304 | tf_op jit(solution)/shard_map/ppermute | solution.py:22
  998.6 34.4 %collective-permute-start.16 = (f32[32,6144]{1,0:T(8,128)}, f32[32,6144]{1,0:T(8,128)}, u32[]{:S(2)}, u32[]{:S(2)}) collective-permute-start(f32[32,6144]{1,0:T(8,128)} %bitcast.69), channel_id=1, source_target_pairs={{0,4},{4,8},{8,12},{12,16},{16,20},{20,24},{24,28},{28,0},{1,5},{5... | collective-permute-start | bytes 2359304 | tf_op jit(solution)/shard_map/ppermute | solution.py:20
  998.6 80.6 %all-to-all-start.4 = ((f32[32,4,1536]{2,0,1:T(8,128)}), f32[32,4,1536]{2,0,1:T(8,128)}, u32[]{:S(2)}, u32[]{:S(2)}) async-start(f32[32,4,1536]{2,0,1:T(8,128)} %get-tuple-element.27), calls=%async_computation.4 | async-start | bytes 1572864 | tf_op jit(solution)/shard_map/all_to_all | solution.py:71
  1075.6 18.6 %copy-start.18 = (f32[128,1536]{1,0:T(8,128)S(1)}, f32[128,1536]{1,0:T(8,128)}, u32[]{:S(2)}) copy-start(f32[128,1536]{1,0:T(8,128)} %copy-done.17) | copy-start | bytes 2359300
  1079.2 15.1 %all-to-all-start.5 = ((f32[32,4,1536]{2,0,1:T(8,128)}), f32[32,4,1536]{2,0,1:T(8,128)S(1)}, u32[]{:S(2)}, u32[]{:S(2)}) async-start(f32[32,4,1536]{2,0,1:T(8,128)} %fusion.93), calls=%async_computation.5 | async-start | bytes 1572864 | tf_op jit(solution)/shard_map/all_to_all | solution.py:71
  1082.7 134.1 %all-reduce.9.cloned.1.call-start = ((), (), s32[]{:S(2)}) async-start(), calls=%async_computation.8 | async-start | bytes 262144 | tf_op jit(solution)/shard_map/psum | solution.py:85
  (16 other events, 98.2 us)
Sparse Core Ops, SparseCore 0:
  344.4 114.7 all-reduce.4
  838.6 115.2 all-reduce.6
  1095.8 120.9 all-reduce.8
where the time goes:
time: 1230 us
  waiting for transfers between devices  628 us (51%)
  matrix products  350 us (28%)
  other arithmetic  73.4 us (6%)
  blocking collectives  59.7 us (5%)
  starting transfers between devices  51.4 us (4%)
  local copies, waits for them, and re-layouts  47.9 us (4%)
  between operations  14.7 us (1%)
    dot_general x9, matrix products, operate(): product = jnp.einsum('nij,knj->nki', blocks, gathered, precision=precise)  299 us
    psum x2, waiting for transfers between devices, body(): gram = lax.psum(gram_part, ('node', 'col'))  230 us
    ppermute x9, waiting for transfers between devices, extended_2(): lax.ppermute(tail, axis, [(i, (i + 1) % count) for i in range(count)])  216 us
    psum x1, waiting for transfers between devices, body(): totals = lax.psum((part,), ('node', 'col'))  121 us
    ppermute x9, waiting for transfers between devices, extended_2(): lax.ppermute(head, axis, [((i + 1) % count, i) for i in range(count)])  51.6 us
    dot_general x9, matrix products, operate(): jnp.einsum('rn,nki->kri', onehot, product, precision=precise)  42.9 us
    ppermute x9, starting transfers between devices, extended_2(): lax.ppermute(head, axis, [((i + 1) % count, i) for i in range(count)])  36.9 us
    gather x9, local copies, waits for them, and re-layouts, operate(): gathered = jnp.take(pieces, lookup, axis=1)  30.9 us
  transfers between devices with their start and end apart: 23, of which 21 were waited for; matrix products, arithmetic and copies ran while one was open for 5% of the time, Pallas kernels for 0%

commit v1 on v0

--- a/solution.py
+++ b/solution.py
@@ -76,7 +76,7 @@
         filtered = chebyshev(basis, operate)
         rows_now = to_rows(filtered)
         gram_part = jnp.dot(rows_now, rows_now.T, precision=precise) / nodes
-        gram = lax.psum(gram_part, ("node", "col"))
+        gram = jnp.sum(lax.all_gather(gram_part, ("node", "col")), axis=0)
         factor = jnp.linalg.cholesky(gram)
         rows_basis = jax.scipy.linalg.solve_triangular(factor, rows_now, lower=True)
         basis = lax.all_to_all(rows_basis, "col", split_axis=0, concat_axis=1, tiled=True)

time: 1230 us -> 1110 us (0.902)
  waiting for transfers between devices: 628 us -> 505 us
    psum x2 -> x0, waiting for transfers between devices: 230 us -> none  [body(): gram = lax.psum(gram_part, ('node', 'col'))]
    all_gather x0 -> x2, waiting for transfers between devices: none -> 107 us  [body(): gram = jnp.sum(lax.all_gather(gram_part, ('node', 'col')), axis=0)]
  transfers between devices with their start and end apart: 23 -> 23, of which waited for: 21 -> 21; matrix products, arithmetic and copies ran while one was open for 5% -> 6% of each run, Pallas kernels for 0% -> 0%
where the time goes in v1:
time: 1110 us; the launch traced here: 1100 us
  waiting for transfers between devices  505 us (45%)
  matrix products  350 us (32%)
  other arithmetic  75.2 us (7%)
  blocking collectives  56.9 us (5%)
  starting transfers between devices  51.5 us (5%)
  local copies, waits for them, and re-layouts  45.3 us (4%)
  between operations  14.7 us (1%)
    dot_general x9, matrix products, operate(): product = jnp.einsum('nij,knj->nki', blocks, gathered, precision=precise)  299 us
    ppermute x9, waiting for transfers between devices, extended_2(): lax.ppermute(tail, axis, [(i, (i + 1) % count) for i in range(count)])  217 us
    psum x1, waiting for transfers between devices, body(): totals = lax.psum((part,), ('node', 'col'))  121 us
    all_gather x2, waiting for transfers between devices, body(): gram = jnp.sum(lax.all_gather(gram_part, ('node', 'col')), axis=0)  107 us
    ppermute x9, waiting for transfers between devices, extended_2(): lax.ppermute(head, axis, [((i + 1) % count, i) for i in range(count)])  51.3 us
    dot_general x9, matrix products, operate(): jnp.einsum('rn,nki->kri', onehot, product, precision=precise)  42.9 us
    ppermute x9, starting transfers between devices, extended_2(): lax.ppermute(head, axis, [((i + 1) % count, i) for i in range(count)])  35.7 us
    gather x9, local copies, waits for them, and re-layouts, operate(): gathered = jnp.take(pieces, lookup, axis=1)  30.9 us
  transfers between devices with their start and end apart: 23, of which 21 were waited for; matrix products, arithmetic and copies ran while one was open for 6% of the time, Pallas kernels for 0%

profile of v1, /device:TPU:0, one launch (start us, length us, event | category | flops | bytes accessed | tf_op | source)
XLA Modules:
  0.0 1099.2 jit_solution(10104638384728532389)
XLA Ops:
  14.1 9.6 reduce_sum.27
  23.9 20.3 %collective-permute-done = f32[32,6144]{1,0:T(8,128)S(1)} collective-permute-done((f32[32,6144]{1,0:T(8,128)}, f32[32,6144]{1,0:T(8,128)S(1)}, u32[]{:S(2)}, u32[]{:S(2)}) %collective-permute-start) | collective-permute-done | bytes 786464 | tf_op jit(solution)/shard_map/ppermute | solution.py:20
  51.4 33.1 %fusion.16 = f32[288,32,128]{2,1,0:T(8,128)S(1)} fusion(f32[288,128,128]{2,1,0:T(8,128)} %param.9, f32[288,32,128]{2,1,0:T(8,128)} %gather_fusion, pred[288]{0:T(512)(128)(4,1)S(1)} %get-tuple-element.10), kind=kOutput, calls=%fused_computation.25 | convolution fusion | flops 1813118976 | bytes 28311840 | tf_op jit(solution)/shard_map/nij,knj->nki/dot_general | solution.py:64
  94.4 29.1 %collective-permute-done.2 = f32[32,6144]{1,0:T(8,128)S(1)} collective-permute-done((f32[32,6144]{1,0:T(8,128)S(1)}, f32[32,6144]{1,0:T(8,128)S(1)}, u32[]{:S(2)}, u32[]{:S(2)}) %collective-permute-start.2) | collective-permute-done | bytes 786464 | tf_op jit(solution)/shard_map/ppermute | solution.py:20
  130.3 33.2 %fusion.14 = f32[288,32,128]{2,1,0:T(8,128)S(1)} fusion(f32[288,128,128]{2,1,0:T(8,128)} %param.9, f32[288,32,128]{2,1,0:T(8,128)} %gather_fusion.1, pred[288]{0:T(512)(128)(4,1)S(1)} %get-tuple-element.10), kind=kOutput, calls=%fused_computation.23 | convolution fusion | flops 1813118976 | bytes 28311840 | tf_op jit(solution)/shard_map/nij,knj->nki/dot_general | solution.py:64
  173.8 28.7 %collective-permute-done.4 = f32[32,6144]{1,0:T(8,128)S(1)} collective-permute-done((f32[32,6144]{1,0:T(8,128)S(1)}, f32[32,6144]{1,0:T(8,128)S(1)}, u32[]{:S(2)}, u32[]{:S(2)}) %collective-permute-start.4) | collective-permute-done | bytes 786464 | tf_op jit(solution)/shard_map/ppermute | solution.py:20
  210.2 33.4 %fusion.12 = f32[288,32,128]{2,1,0:T(8,128)S(1)} fusion(f32[288,128,128]{2,1,0:T(8,128)} %param.9, f32[288,32,128]{2,1,0:T(8,128)} %gather_fusion.2, pred[288]{0:T(512)(128)(4,1)S(1)} %get-tuple-element.10), kind=kOutput, calls=%fused_computation.21 | convolution fusion | flops 1813118976 | bytes 28311840 | tf_op jit(solution)/shard_map/nij,knj->nki/dot_general | solution.py:64
  253.9 28.5 %collective-permute-done.6 = f32[32,6144]{1,0:T(8,128)S(1)} collective-permute-done((f32[32,6144]{1,0:T(8,128)S(1)}, f32[32,6144]{1,0:T(8,128)S(1)}, u32[]{:S(2)}, u32[]{:S(2)}) %collective-permute-start.6) | collective-permute-done | bytes 786464 | tf_op jit(solution)/shard_map/ppermute | solution.py:20
  290.2 33.2 %fusion.10 = f32[288,32,128]{2,1,0:T(8,128)S(1)} fusion(f32[288,128,128]{2,1,0:T(8,128)} %param.9, f32[288,32,128]{2,1,0:T(8,128)} %gather_fusion.3, pred[288]{0:T(512)(128)(4,1)S(1)} %get-tuple-element.10), kind=kOutput, calls=%fused_computation.19 | convolution fusion | flops 1813118976 | bytes 28311840 | tf_op jit(solution)/shard_map/nij,knj->nki/dot_general | solution.py:64
  328.6 14.2 %all_to_all.105 = f32[32,4,1536]{2,0,1:T(8,128)S(1)} all-to-all(f32[32,4,1536]{2,0,1:T(8,128)S(1)} %bitcast.289), channel_id=1, replica_groups=mesh['node'=8,'col'=4] {'col'}, dimensions={1} | all-to-all | bytes 1572864 | tf_op jit(solution)/shard_map/all_to_all | solution.py:71
  344.6 53.5 %all-gather.5.cloned.1.call-done = f32[4096,128]{1,0:T(8,128)} async-done(((f32[128,128]{1,0:T(8,128)}), f32[4096,128]{1,0:T(8,128)}) %all-gather.5.cloned.1.call-update) | async-done | bytes 2097168 | tf_op jit(solution)/shard_map/all_gather | solution.py:79
  399.9 11.7 %cholesky.44 = f32[128,128]{1,0:T(8,128)S(1)} custom-call(f32[128,128]{1,0:T(8,128)S(1)} %fusion.125), custom_call_target="Cholesky" | custom-call | tf_op jit(solution)/shard_map/jit(cholesky)/cholesky | solution.py:80
  413.0 9.8 custom-call.6
  423.6 14.2 %all_to_all.106 = f32[4,32,1536]{2,1,0:T(8,128)S(1)} all-to-all(f32[4,32,1536]{2,1,0:T(8,128)S(1)} %bitcast.282), channel_id=1, replica_groups=mesh['node'=8,'col'=4] {'col'}, dimensions={0} | all-to-all | bytes 1572864 | tf_op jit(solution)/shard_map/all_to_all | solution.py:82
  444.2 28.4 %collective-permute-done.8 = f32[32,6144]{1,0:T(8,128)} collective-permute-done((f32[32,6144]{1,0:T(8,128)S(1)}, f32[32,6144]{1,0:T(8,128)}, u32[]{:S(2)}, u32[]{:S(2)}) %collective-permute-start.8) | collective-permute-done | bytes 786464 | tf_op jit(solution)/shard_map/ppermute | solution.py:20
  478.9 33.1 %fusion.8 = f32[288,32,128]{2,1,0:T(8,128)S(1)} fusion(f32[288,128,128]{2,1,0:T(8,128)} %param.9, f32[288,32,128]{2,1,0:T(8,128)} %gather_fusion.4, pred[288]{0:T(512)(128)(4,1)S(1)} %get-tuple-element.10), kind=kOutput, calls=%fused_computation.17 | convolution fusion | flops 1813118976 | bytes 28311840 | tf_op jit(solution)/shard_map/nij,knj->nki/dot_general | solution.py:64
  521.9 28.8 %collective-permute-done.10 = f32[32,6144]{1,0:T(8,128)S(1)} collective-permute-done((f32[32,6144]{1,0:T(8,128)S(1)}, f32[32,6144]{1,0:T(8,128)S(1)}, u32[]{:S(2)}, u32[]{:S(2)}) %collective-permute-start.10) | collective-permute-done | bytes 786464 | tf_op jit(solution)/shard_map/ppermute | solution.py:20
  556.8 33.2 %fusion.6 = f32[288,32,128]{2,1,0:T(8,128)S(1)} fusion(f32[288,128,128]{2,1,0:T(8,128)} %param.9, f32[288,32,128]{2,1,0:T(8,128)} %gather_fusion.5, pred[288]{0:T(512)(128)(4,1)S(1)} %get-tuple-element.10), kind=kOutput, calls=%fused_computation.15 | convolution fusion | flops 1813118976 | bytes 28311840 | tf_op jit(solution)/shard_map/nij,knj->nki/dot_general | solution.py:64
  600.3 27.3 %collective-permute-done.12 = f32[32,6144]{1,0:T(8,128)S(1)} collective-permute-done((f32[32,6144]{1,0:T(8,128)S(1)}, f32[32,6144]{1,0:T(8,128)S(1)}, u32[]{:S(2)}, u32[]{:S(2)}) %collective-permute-start.12) | collective-permute-done | bytes 786464 | tf_op jit(solution)/shard_map/ppermute | solution.py:20
  635.3 33.5 %fusion.4 = f32[288,32,128]{2,1,0:T(8,128)S(1)} fusion(f32[288,128,128]{2,1,0:T(8,128)} %param.9, f32[288,32,128]{2,1,0:T(8,128)} %gather_fusion.6, pred[288]{0:T(512)(128)(4,1)S(1)} %get-tuple-element.10), kind=kOutput, calls=%fused_computation.13 | convolution fusion | flops 1813118976 | bytes 28311840 | tf_op jit(solution)/shard_map/nij,knj->nki/dot_general | solution.py:64
  682.0 25.7 %collective-permute-done.14 = f32[32,6144]{1,0:T(8,128)} collective-permute-done((f32[32,6144]{1,0:T(8,128)S(1)}, f32[32,6144]{1,0:T(8,128)}, u32[]{:S(2)}, u32[]{:S(2)}) %collective-permute-start.14) | collective-permute-done | bytes 786464 | tf_op jit(solution)/shard_map/ppermute | solution.py:20
  717.4 33.2 %fusion.2 = f32[288,32,128]{2,1,0:T(8,128)S(1)} fusion(f32[288,128,128]{2,1,0:T(8,128)} %param.9, f32[288,32,128]{2,1,0:T(8,128)} %gather_fusion.7, pred[288]{0:T(512)(128)(4,1)S(1)} %get-tuple-element.10), kind=kOutput, calls=%fused_computation.11 | convolution fusion | flops 1813118976 | bytes 28311840 | tf_op jit(solution)/shard_map/nij,knj->nki/dot_general | solution.py:64
  760.1 14.3 %all_to_all.107 = f32[32,4,1536]{2,0,1:T(8,128)S(1)} all-to-all(f32[32,4,1536]{2,0,1:T(8,128)S(1)} %get-tuple-element.13), channel_id=1, replica_groups=mesh['node'=8,'col'=4] {'col'}, dimensions={1} | all-to-all | bytes 1572864 | tf_op jit(solution)/shard_map/all_to_all | solution.py:71
  775.9 53.6 %all-gather.7.cloned.1.call-done = f32[4096,128]{1,0:T(8,128)} async-done(((f32[128,128]{1,0:T(8,128)}), f32[4096,128]{1,0:T(8,128)}) %all-gather.7.cloned.1.call-update) | async-done | bytes 2097168 | tf_op jit(solution)/shard_map/all_gather | solution.py:79
  831.2 11.7 %cholesky.55 = f32[128,128]{1,0:T(8,128)S(1)} custom-call(f32[128,128]{1,0:T(8,128)S(1)} %fusion.122), custom_call_target="Cholesky" | custom-call | tf_op jit(solution)/shard_map/jit(cholesky)/cholesky | solution.py:80
  844.3 9.8 custom-call.7
  855.0 14.2 %all_to_all.108 = f32[4,32,1536]{2,1,0:T(8,128)S(1)} all-to-all(f32[4,32,1536]{2,1,0:T(8,128)S(1)} %bitcast.283), channel_id=1, replica_groups=mesh['node'=8,'col'=4] {'col'}, dimensions={0} | all-to-all | bytes 1572864 | tf_op jit(solution)/shard_map/all_to_all | solution.py:82
  878.8 27.3 %collective-permute-done.17 = f32[32,6144]{1,0:T(8,128)} collective-permute-done((f32[32,6144]{1,0:T(8,128)}, f32[32,6144]{1,0:T(8,128)}, u32[]{:S(2)}, u32[]{:S(2)}) %collective-permute-start.17) | collective-permute-done | bytes 786464 | tf_op jit(solution)/shard_map/ppermute | solution.py:22
  912.1 33.1 %fusion = f32[288,32,128]{2,1,0:T(8,128)S(1)} fusion(f32[288,128,128]{2,1,0:T(8,128)} %param.9, f32[288,32,128]{2,1,0:T(8,128)} %gather_fusion.8, pred[288]{0:T(512)(128)(4,1)S(1)} %get-tuple-element.10), kind=kOutput, calls=%fused_computation.9 | convolution fusion | flops 1813118976 | bytes 28311840 | tf_op jit(solution)/shard_map/nij,knj->nki/dot_general | solution.py:64
  945.3 4.8 fusion.66
  959.7 9.0 all-to-all-done.5
  970.1 120.9 %all-reduce.3.cloned.1.call-done = (f32[128,128]{1,0:T(8,128)}, f32[128,128]{1,0:T(8,128)}) async-done(((f32[128,128]{1,0:T(8,128)}, f32[128,128]{1,0:T(8,128)}), (f32[128,128]{1,0:T(8,128)}, f32[128,128]{1,0:T(8,128)})) %all-reduce.3.cloned.1.call-update) | async-done | bytes 131088 | tf_op jit(solution)/shard_map/psum | solution.py:85
  (165 shorter events, 190.2 us)
Async XLA Ops:
  7.2 390.9 %all-gather.5.cloned.1.call-start = ((), (), s32[]{:S(2)}) async-start(), calls=%async_computation.6 | async-start | bytes 2162688 | tf_op jit(solution)/shard_map/all_gather | solution.py:79
  7.2 37.0 %collective-permute-start = (f32[32,6144]{1,0:T(8,128)}, f32[32,6144]{1,0:T(8,128)S(1)}, u32[]{:S(2)}, u32[]{:S(2)}) collective-permute-start(f32[32,6144]{1,0:T(8,128)} %param.12), channel_id=1, source_target_pairs={{0,4},{4,8},{8,12},{12,16},{16,20},{20,24},{24,28},{28,0},{1,5},{5... | collective-permute-start | bytes 2359304 | tf_op jit(solution)/shard_map/ppermute | solution.py:20
  10.2 36.2 %collective-permute-start.1 = (f32[32,6144]{1,0:T(8,128)}, f32[32,6144]{1,0:T(8,128)}, u32[]{:S(2)}, u32[]{:S(2)}) collective-permute-start(f32[32,6144]{1,0:T(8,128)} %param.12), channel_id=1, source_target_pairs={{4,0},{8,4},{12,8},{16,12},{20,16},{24,20},{28,24},{0,28},{5,1},{9... | collective-permute-start | bytes 2359304 | tf_op jit(solution)/shard_map/ppermute | solution.py:22
  14.0 32.4 %copy-start = (f32[32,6144]{1,0:T(8,128)S(1)}, f32[32,6144]{1,0:T(8,128)}, u32[]{:S(2)}) copy-start(f32[32,6144]{1,0:T(8,128)} %param.12) | copy-start | bytes 2359300
  89.3 34.3 %copy-start.7 = (f32[32,128,48]{1,2,0:T(8,128)}, f32[32,128,48]{1,2,0:T(8,128)S(1)}, u32[]{:S(2)}) copy-start(f32[32,128,48]{1,2,0:T(8,128)S(1)} %fusion.34) | copy-start | bytes 2359300
  89.7 33.9 %collective-permute-start.2 = (f32[32,6144]{1,0:T(8,128)S(1)}, f32[32,6144]{1,0:T(8,128)S(1)}, u32[]{:S(2)}, u32[]{:S(2)}) collective-permute-start(f32[32,6144]{1,0:T(8,128)S(1)} %broadcast_multiply_fusion.1), channel_id=1, source_target_pairs={{0,4},{4,8},{8,12},{12,16},{16,20},{20,24},{24,28},{28,0},{1,5},{5... | collective-permute-start | bytes 2359304 | tf_op jit(solution)/shard_map/ppermute | solution.py:20
  90.8 35.9 %collective-permute-start.3 = (f32[32,6144]{1,0:T(8,128)S(1)}, f32[32,6144]{1,0:T(8,128)S(1)}, u32[]{:S(2)}, u32[]{:S(2)}) collective-permute-start(f32[32,6144]{1,0:T(8,128)S(1)} %broadcast_multiply_fusion.1), channel_id=1, source_target_pairs={{4,0},{8,4},{12,8},{16,12},{20,16},{24,20},{28,24},{0,28},{5,1},{9... | collective-permute-start | bytes 2359304 | tf_op jit(solution)/shard_map/ppermute | solution.py:22
  169.0 37.3 %copy-start.10 = (f32[32,6144]{1,0:T(8,128)}, f32[32,6144]{1,0:T(8,128)S(1)}, u32[]{:S(2)}) copy-start(f32[32,6144]{1,0:T(8,128)S(1)} %fusion.90) | copy-start | bytes 2359300
  169.0 33.5 %collective-permute-start.4 = (f32[32,6144]{1,0:T(8,128)S(1)}, f32[32,6144]{1,0:T(8,128)S(1)}, u32[]{:S(2)}, u32[]{:S(2)}) collective-permute-start(f32[32,6144]{1,0:T(8,128)S(1)} %fusion.90), channel_id=1, source_target_pairs={{0,4},{4,8},{8,12},{12,16},{16,20},{20,24},{24,28},{28,0},{1,5},{5... | collective-permute-start | bytes 2359304 | tf_op jit(solution)/shard_map/ppermute | solution.py:20
  169.1 37.2 %collective-permute-start.5 = (f32[32,6144]{1,0:T(8,128)S(1)}, f32[32,6144]{1,0:T(8,128)S(1)}, u32[]{:S(2)}, u32[]{:S(2)}) collective-permute-start(f32[32,6144]{1,0:T(8,128)S(1)} %fusion.90), channel_id=1, source_target_pairs={{4,0},{8,4},{12,8},{16,12},{20,16},{24,20},{28,24},{0,28},{5,1},{9... | collective-permute-start | bytes 2359304 | tf_op jit(solution)/shard_map/ppermute | solution.py:22
  249.1 37.3 %copy-start.19 = (f32[32,6144]{1,0:T(8,128)}, f32[32,6144]{1,0:T(8,128)S(1)}, u32[]{:S(2)}) copy-start(f32[32,6144]{1,0:T(8,128)S(1)} %fusion.86) | copy-start | bytes 2359300
  249.1 33.3 %collective-permute-start.6 = (f32[32,6144]{1,0:T(8,128)S(1)}, f32[32,6144]{1,0:T(8,128)S(1)}, u32[]{:S(2)}, u32[]{:S(2)}) collective-permute-start(f32[32,6144]{1,0:T(8,128)S(1)} %fusion.86), channel_id=1, source_target_pairs={{0,4},{4,8},{8,12},{12,16},{16,20},{20,24},{24,28},{28,0},{1,5},{5... | collective-permute-start | bytes 2359304 | tf_op jit(solution)/shard_map/ppermute | solution.py:20
  249.2 37.2 %collective-permute-start.7 = (f32[32,6144]{1,0:T(8,128)S(1)}, f32[32,6144]{1,0:T(8,128)S(1)}, u32[]{:S(2)}, u32[]{:S(2)}) collective-permute-start(f32[32,6144]{1,0:T(8,128)S(1)} %fusion.86), channel_id=1, source_target_pairs={{4,0},{8,4},{12,8},{16,12},{20,16},{24,20},{28,24},{0,28},{5,1},{9... | collective-permute-start | bytes 2359304 | tf_op jit(solution)/shard_map/ppermute | solution.py:22
  344.3 485.1 %all-gather.7.cloned.1.call-start = ((), (), s32[]{:S(2)}) async-start(), calls=%async_computation.7 | async-start | bytes 2162688 | tf_op jit(solution)/shard_map/all_gather | solution.py:79
  437.9 37.4 %copy-start.3 = (f32[4,4,8,1536]{3,2,0,1:T(8,128)}, f32[4,4,8,1536]{3,2,0,1:T(8,128)S(1)}, u32[]{:S(2)}) copy-start(f32[4,4,8,1536]{3,2,0,1:T(8,128)S(1)} %copy.134) | copy-start | bytes 2359300
  437.9 34.7 %collective-permute-start.8 = (f32[32,6144]{1,0:T(8,128)S(1)}, f32[32,6144]{1,0:T(8,128)}, u32[]{:S(2)}, u32[]{:S(2)}) collective-permute-start(f32[32,6144]{1,0:T(8,128)S(1)} %bitcast.271), channel_id=1, source_target_pairs={{0,4},{4,8},{8,12},{12,16},{16,20},{20,24},{24,28},{28,0},{1,5},{5... | collective-permute-start | bytes 2359304 | tf_op jit(solution)/shard_map/ppermute | solution.py:20
  439.3 35.9 %collective-permute-start.9 = (f32[32,6144]{1,0:T(8,128)S(1)}, f32[32,6144]{1,0:T(8,128)S(1)}, u32[]{:S(2)}, u32[]{:S(2)}) collective-permute-start(f32[32,6144]{1,0:T(8,128)S(1)} %bitcast.272), channel_id=1, source_target_pairs={{4,0},{8,4},{12,8},{16,12},{20,16},{24,20},{28,24},{0,28},{5,1},{9... | collective-permute-start | bytes 2359304 | tf_op jit(solution)/shard_map/ppermute | solution.py:22
  517.1 33.6 %collective-permute-start.10 = (f32[32,6144]{1,0:T(8,128)S(1)}, f32[32,6144]{1,0:T(8,128)S(1)}, u32[]{:S(2)}, u32[]{:S(2)}) collective-permute-start(f32[32,6144]{1,0:T(8,128)S(1)} %broadcast_multiply_fusion), channel_id=1, source_target_pairs={{0,4},{4,8},{8,12},{12,16},{16,20},{20,24},{24,28},{28,0},{1,5},{5... | collective-permute-start | bytes 2359304 | tf_op jit(solution)/shard_map/ppermute | solution.py:20
  518.4 34.6 %collective-permute-start.11 = (f32[32,6144]{1,0:T(8,128)S(1)}, f32[32,6144]{1,0:T(8,128)S(1)}, u32[]{:S(2)}, u32[]{:S(2)}) collective-permute-start(f32[32,6144]{1,0:T(8,128)S(1)} %broadcast_multiply_fusion), channel_id=1, source_target_pairs={{4,0},{8,4},{12,8},{16,12},{20,16},{24,20},{28,24},{0,28},{5,1},{9... | collective-permute-start | bytes 2359304 | tf_op jit(solution)/shard_map/ppermute | solution.py:22
  594.8 32.8 %copy-start.13 = (f32[32,128,48]{1,2,0:T(8,128)}, f32[32,128,48]{1,2,0:T(8,128)S(1)}, u32[]{:S(2)}) copy-start(f32[32,128,48]{1,2,0:T(8,128)S(1)} %fusion.24) | copy-start | bytes 2359300
  595.5 32.1 %collective-permute-start.12 = (f32[32,6144]{1,0:T(8,128)S(1)}, f32[32,6144]{1,0:T(8,128)S(1)}, u32[]{:S(2)}, u32[]{:S(2)}) collective-permute-start(f32[32,6144]{1,0:T(8,128)S(1)} %fusion.76), channel_id=1, source_target_pairs={{0,4},{4,8},{8,12},{12,16},{16,20},{20,24},{24,28},{28,0},{1,5},{5... | collective-permute-start | bytes 2359304 | tf_op jit(solution)/shard_map/ppermute | solution.py:20
  595.8 35.5 %collective-permute-start.13 = (f32[32,6144]{1,0:T(8,128)S(1)}, f32[32,6144]{1,0:T(8,128)S(1)}, u32[]{:S(2)}, u32[]{:S(2)}) collective-permute-start(f32[32,6144]{1,0:T(8,128)S(1)} %fusion.76), channel_id=1, source_target_pairs={{4,0},{8,4},{12,8},{16,12},{20,16},{24,20},{28,24},{0,28},{5,1},{9... | collective-permute-start | bytes 2359304 | tf_op jit(solution)/shard_map/ppermute | solution.py:22
  674.6 33.0 %copy-start.21 = (f32[32,6144]{1,0:T(8,128)}, f32[32,6144]{1,0:T(8,128)S(1)}, u32[]{:S(2)}) copy-start(f32[32,6144]{1,0:T(8,128)S(1)} %fusion.72) | copy-start | bytes 2359300
  674.6 33.0 %collective-permute-start.14 = (f32[32,6144]{1,0:T(8,128)S(1)}, f32[32,6144]{1,0:T(8,128)}, u32[]{:S(2)}, u32[]{:S(2)}) collective-permute-start(f32[32,6144]{1,0:T(8,128)S(1)} %fusion.72), channel_id=1, source_target_pairs={{0,4},{4,8},{8,12},{12,16},{16,20},{20,24},{24,28},{28,0},{1,5},{5... | collective-permute-start | bytes 2359304 | tf_op jit(solution)/shard_map/ppermute | solution.py:20
  674.7 37.3 %collective-permute-start.15 = (f32[32,6144]{1,0:T(8,128)S(1)}, f32[32,6144]{1,0:T(8,128)}, u32[]{:S(2)}, u32[]{:S(2)}) collective-permute-start(f32[32,6144]{1,0:T(8,128)S(1)} %fusion.72), channel_id=1, source_target_pairs={{4,0},{8,4},{12,8},{16,12},{20,16},{24,20},{28,24},{0,28},{5,1},{9... | collective-permute-start | bytes 2359304 | tf_op jit(solution)/shard_map/ppermute | solution.py:22
  855.0 23.9 %copy-start.17 = (f32[128,1536]{1,0:T(8,128)}, f32[128,1536]{1,0:T(8,128)S(1)}, u32[]{:S(2)}) copy-start(f32[128,1536]{1,0:T(8,128)S(1)} %fusion.120) | copy-start | bytes 2359300
  870.1 36.1 %collective-permute-start.17 = (f32[32,6144]{1,0:T(8,128)}, f32[32,6144]{1,0:T(8,128)}, u32[]{:S(2)}, u32[]{:S(2)}) collective-permute-start(f32[32,6144]{1,0:T(8,128)} %bitcast.71), channel_id=1, source_target_pairs={{4,0},{8,4},{12,8},{16,12},{20,16},{24,20},{28,24},{0,28},{5,1},{9... | collective-permute-start | bytes 2359304 | tf_op jit(solution)/shard_map/ppermute | solution.py:22
  873.1 34.3 %collective-permute-start.16 = (f32[32,6144]{1,0:T(8,128)}, f32[32,6144]{1,0:T(8,128)}, u32[]{:S(2)}, u32[]{:S(2)}) collective-permute-start(f32[32,6144]{1,0:T(8,128)} %bitcast.71), channel_id=1, source_target_pairs={{0,4},{4,8},{8,12},{12,16},{16,20},{20,24},{24,28},{28,0},{1,5},{5... | collective-permute-start | bytes 2359304 | tf_op jit(solution)/shard_map/ppermute | solution.py:20
  873.1 80.5 %all-to-all-start.4 = ((f32[32,4,1536]{2,0,1:T(8,128)}), f32[32,4,1536]{2,0,1:T(8,128)}, u32[]{:S(2)}, u32[]{:S(2)}) async-start(f32[32,4,1536]{2,0,1:T(8,128)} %get-tuple-element.12), calls=%async_computation.4 | async-start | bytes 1572864 | tf_op jit(solution)/shard_map/all_to_all | solution.py:71
  950.1 18.6 %copy-start.18 = (f32[128,1536]{1,0:T(8,128)S(1)}, f32[128,1536]{1,0:T(8,128)}, u32[]{:S(2)}) copy-start(f32[128,1536]{1,0:T(8,128)} %copy-done.17) | copy-start | bytes 2359300
  953.6 15.1 %all-to-all-start.5 = ((f32[32,4,1536]{2,0,1:T(8,128)}), f32[32,4,1536]{2,0,1:T(8,128)S(1)}, u32[]{:S(2)}, u32[]{:S(2)}) async-start(f32[32,4,1536]{2,0,1:T(8,128)} %fusion.93), calls=%async_computation.5 | async-start | bytes 1572864 | tf_op jit(solution)/shard_map/all_to_all | solution.py:71
  957.1 134.0 %all-reduce.3.cloned.1.call-start = ((), (), s32[]{:S(2)}) async-start(), calls=%async_computation.8 | async-start | bytes 262144 | tf_op jit(solution)/shard_map/psum | solution.py:85
  (16 other events, 96.9 us)
Sparse Core Ops, SparseCore 0:
  344.4 53.6 all-gather.4
  776.0 53.4 all-gather.6
  970.3 120.7 all-reduce.2
